TPU v7x, 512 devices: a whole 4x4x16 slice. The times are simulated.
512 devices in a mesh: stream: 32 (over z, x_hi), span: 16 (over y, x_lo, core).
Axes of the slice: x: 4 (x_hi: 2, x_lo: 2; x = x_hi * 2 + x_lo), y: 4, z: 16, core: 2. Of those that a mesh axis runs over, the one named last changes fastest.
Arguments:
- checkpoint: float32 [5, 192, 32, 2048], P(None, None, 'stream', 'span'), may hold values from -4.8 to 4.8
- adjoint: float32 [5, 192, 32, 2048], P(None, None, 'stream', 'span'), may hold values from -6 to 6
- line_inverse: bfloat16 [32, 3, 320, 320], P('stream'), may hold values from -0.3125 to 0.3125
- row_source: int32 [3072], replicated, may hold values from 0 to 3071, as said below
Outputs:
- adjoint_start: float32 [5, 192, 32, 2048], P(None, None, 'stream', 'span')
Inputs may be any that keep to these rules, and one draw needn't show every extreme that they name: `row_source`: every rotor outlet row is taken by exactly one stator inlet row, and each stator span tile takes exactly 12 rows from each rotor span tile.
All inputs are finite; a program needn't handle non-finite values.
Results may differ from a plain program's by a relative error of at most 0.0029.
Values sent between devices are 32-bit elements; how exact they have to be, the bound alone decides.
A program may use at most 64 MiB of HBM per device.

v0:
```python
import jax
import jax.numpy as jnp
from jax import lax
from jax.sharding import PartitionSpec as P

time_step = 0.5
ADVECTION = (1.0, 0.6, 0.8, 1.2, 0.7)
DISSIPATION = (0.3, 0.25, 0.35, 0.3, 0.4)
SPREADING = (0.4, 0.3, 0.5, 0.35, 0.45)


def with_halo(block, sides, width):
    for axis, dim in sides:
        count = lax.axis_size(axis)
        forward = [(i, i + 1) for i in range(count - 1)]
        forward.append((count - 1, 0))
        backward = [(target, source) for source, target in forward]
        low = lax.ppermute(
            lax.slice_in_dim(block, block.shape[dim] - width, None, axis=dim), axis, forward
        )
        high = lax.ppermute(lax.slice_in_dim(block, 0, width, axis=dim), axis, backward)
        block = jnp.concatenate([low, block, high], axis=dim)
    return block


def per_state(values):
    return jnp.array(values, jnp.float32).reshape(5, 1, 1, 1)


def plane_remap(lower_rim, upper_rim, row_source):
    span_count = lax.axis_size("span")
    position = lax.axis_index("span")
    line_points = lower_rim.shape[1]
    capacity = line_points // span_count
    src_dev = (row_source // line_points).reshape(span_count, line_points)
    src_row = (row_source % line_points).reshape(span_count, line_points)
    devices = jnp.arange(span_count, dtype=jnp.int32)
    slot_ids = jnp.arange(capacity, dtype=jnp.int32)
    point_ids = jnp.arange(line_points, dtype=jnp.int32)
    onehot = (src_dev[:, :, None] == devices[None, None, :]).astype(jnp.int32)
    arrival = jnp.sum((jnp.cumsum(onehot, axis=1) - onehot) * onehot, axis=2)
    pick_lower = (
        (src_dev == position)[:, :, None] & (arrival[:, :, None] == slot_ids[None, None, :])
    ).astype(jnp.int32)
    send_lower = jnp.sum(pick_lower * src_row[:, :, None], axis=1).reshape(span_count * capacity)
    own_dev = lax.dynamic_index_in_dim(src_dev, position, 0, keepdims=False)
    own_arrival = lax.dynamic_index_in_dim(arrival, position, 0, keepdims=False)
    pick_upper = (
        (own_dev[None, :] == devices[:, None])[:, :, None]
        & (own_arrival[None, :, None] == slot_ids[None, None, :])
    ).astype(jnp.int32)
    send_upper = jnp.sum(pick_upper * point_ids[None, :, None], axis=1).reshape(
        span_count * capacity
    )
    outgoing = (jnp.take(lower_rim, send_lower, axis=1), jnp.take(upper_rim, send_upper, axis=1))
    got_lower, got_upper = (
        lax.all_to_all(outgoing[0], "span", split_axis=1, concat_axis=1, tiled=True),
        lax.all_to_all(outgoing[1], "span", split_axis=1, concat_axis=1, tiled=True),
    )
    lower_mapped = jnp.take(got_lower, own_dev * capacity + own_arrival, axis=1)
    matches = (
        (src_dev == position)[:, :, None] & (src_row[:, :, None] == point_ids[None, None, :])
    ).astype(jnp.int32)
    where_from = devices[:, None] * capacity + arrival
    upper_pos = jnp.sum(matches * where_from[:, :, None], axis=(0, 1))
    upper_mapped = jnp.take(got_upper, upper_pos, axis=1)
    return (lower_mapped, upper_mapped)


def gather_rims(field, row_source):
    stream_count = lax.axis_size("stream")
    stream_place = lax.axis_index("stream")
    halfway = stream_count // 2
    padded = with_halo(field, (("stream", 2), ("span", 3)), 1)
    lower_rim = padded[:, :, 0, 1:-1]
    upper_rim = padded[:, :, -1, 1:-1]
    left_rim = padded[:, :, 1:-1, :-2]
    right_rim = padded[:, :, 1:-1, 2:]
    lower_rim = jnp.where(stream_place == 0, 0.0, lower_rim)
    upper_rim = jnp.where(stream_place == stream_count - 1, 0.0, upper_rim)
    lower_mapped, upper_mapped = plane_remap(lower_rim, upper_rim, row_source)
    lower_rim = jnp.where(stream_place == halfway, lower_mapped, lower_rim)
    upper_rim = jnp.where(stream_place == halfway - 1, upper_mapped, upper_rim)
    return (lower_rim, upper_rim, left_rim, right_rim)


def apply_operator(field, rims, coef_down, coef_up, center, lateral):
    lower_rim, upper_rim, left_rim, right_rim = rims
    upstream = jnp.concatenate([lower_rim[:, :, None], field[:, :, :-1]], axis=2)
    downstream = jnp.concatenate([field[:, :, 1:], upper_rim[:, :, None]], axis=2)
    lateral_sum = left_rim + right_rim - 2.0 * field
    return coef_down * downstream + coef_up * upstream + center * field + lateral * lateral_sum


def local(checkpoint, adjoint, line_inverse, row_source):
    advect = per_state(ADVECTION)
    dissip = per_state(DISSIPATION)
    lateral = per_state(SPREADING)
    toward_down = -0.5 * advect + dissip
    toward_up = 0.5 * advect + dissip
    center = -2.0 * dissip
    flux = jnp.tanh(checkpoint)
    flux_rims = gather_rims(flux, row_source)
    advanced = checkpoint + time_step * apply_operator(
        flux, flux_rims, toward_down, toward_up, center, lateral
    )
    tanh_adv = jnp.tanh(advanced)
    section_slope = 2.0 - tanh_adv * tanh_adv
    line_points = checkpoint.shape[1]
    stations = checkpoint.shape[2]
    span_cells = checkpoint.shape[3]
    blocks = line_inverse.shape[1]
    block_points = line_points // blocks
    rounded = adjoint.astype(jnp.bfloat16).reshape(5, blocks, block_points, stations, span_cells)
    inverse = line_inverse.reshape(stations, blocks, 5, block_points, 5, block_points)
    carried = jnp.einsum(
        "sbclem,cblsp->ebmsp", inverse, rounded, preferred_element_type=jnp.float32
    ).reshape(5, line_points, stations, span_cells)
    weighted = section_slope * carried
    weight_rims = gather_rims(weighted, row_source)
    tangent = 1.0 - flux * flux
    return weighted + time_step * tangent * apply_operator(
        weighted, weight_rims, toward_up, toward_down, center, lateral
    )


def solution(mesh):
    return jax.shard_map(
        local,
        mesh=mesh,
        in_specs=(
            P(None, None, "stream", "span"),
            P(None, None, "stream", "span"),
            P("stream", None, None, None),
            P(),
        ),
        out_specs=P(None, None, "stream", "span"),
        check_vma=False,
    )
```

profile of v0, /device:TPU:4, one launch (start us, length us, event | category | flops | bytes accessed | tf_op | source)
XLA Modules:
  0.0 159.7 jit_solution(2668991006154800796)
XLA Ops:
  0.0 1.9 %tanh_bitcast_fusion = (f32[5,192,1,128]{3,1,2,0:T(8,128)}, f32[5,192,1,128]{3,1,0,2:T(8,128)S(1)}) fusion(f32[5,192,1,128]{3,1,0,2:T(8,128)} %bitcast.151), kind=kLoop, calls=%fused_computation.113 | loop fusion | bytes 1474560 | tf_op jit(solution)/shard_map/tanh | solution.py:102
  1.9 7.8 %collective-permute-start = (f32[5,192,1,128]{3,1,2,0:T(8,128)}, f32[5,192,1,128]{3,1,2,0:T(8,128)S(1)}, u32[]{:S(2)}, u32[]{:S(2)}) collective-permute-start(f32[5,192,1,128]{3,1,2,0:T(8,128)} %get-tuple-element.12), channel_id=1, source_target_pairs={{16,0},{32,16},{48,32},{64,48},{80,64},{96,80},{112,96},{128,112},... | collective-permute-start | bytes 1474568 | tf_op jit(solution)/shard_map/ppermute | solution.py:21
  9.7 1.9 %collective-permute-start.1 = (f32[5,192,1,128]{3,1,2,0:T(8,128)}, f32[5,192,1,128]{3,1,2,0:T(8,128)S(1)}, u32[]{:S(2)}, u32[]{:S(2)}) collective-permute-start(f32[5,192,1,128]{3,1,2,0:T(8,128)} %get-tuple-element.12), channel_id=1, source_target_pairs={{0,16},{16,32},{32,48},{48,64},{64,80},{80,96},{96,112},{112,128},... | collective-permute-start | bytes 1474568 | tf_op jit(solution)/shard_map/ppermute | solution.py:18
  11.9 9.1 %reduce-window.6 = s32[16,16,2,128]{3,1,2,0:T(8,128)S(1)} reduce-window(s32[16,16,2,128]{3,1,2,0:T(8,128)S(1)} %copy_bitcast_fusion, s32[]{:T(128)} %constant.84.clone.1), window={size=1x1x1x128 pad=0_0x0_0x0_0x127_0}, to_apply=%region_0.1 | reduce-window | flops 8323072 | bytes 524292 | tf_op jit(solution)/shard_map/reduce-window
  22.8 2.5 %reshape.161 = bf16[3,5,64,5,64]{4,3,2,1,0:T(8,128)(2,1)S(1)} reshape(bf16[1,3,320,320]{3,2,1,0:T(8,128)(2,1)} %param.11) | data formatting | bytes 1228800 | tf_op jit(solution)/shard_map/reshape.24
  25.3 1.4 convert_element_type.6
  27.5 1.7 %select_reduce_fusion = s32[192]{0:T(256)S(1)} fusion(s32[16,192]{1,0:T(8,128)S(1)} %broadcast_add_fusion, s32[16,192]{1,0:T(8,128)S(1)} %eq.175, pred[16,192]{1,0:T(8,128)(4,1)S(1)} %broadcast_compare_fusion), kind=kLoop, calls=%fused_computation.8 | loop fusion | flops 2359104 | bytes 28416 | tf_op jit(solution)/shard_map/reduce_sum | solution.py:65
  29.2 2.2 %fusion.3 = f32[5,3,64,1,128]{4,2,0,1,3:T(8,128)} fusion(bf16[3,5,64,5,64]{4,3,2,1,0:T(8,128)(2,1)S(1)} %reshape.161, bf16[5,3,64,128,1]{3,2,1,0,4:T(8,128)(2,1)} %bitcast.159), kind=kOutput, calls=%fused_computation.15 | convolution fusion | flops 78643200 | bytes 1351680 | tf_op jit(solution)/shard_map/sbclem,cblsp->ebmsp/dot_general | solution.py:116
  33.9 3.7 %all-to-all-start.1 = ((f32[5,192,128]{2,0,1:T(8,128)}), f32[5,192,128]{2,0,1:T(8,128)S(1)}, u32[]{:S(2)}, u32[]{:S(2)}) async-start(f32[5,192,128]{2,0,1:T(8,128)} %select_bitcast_fusion.2), calls=%async_computation.1 | async-start | bytes 1572864 | tf_op jit(solution)/shard_map/all_to_all | solution.py:57
  38.0 1.8 %gather_fusion = f32[192,5,128]{2,1,0:T(8,128)} fusion(f32[5,192,128]{2,0,1:T(8,128)S(1)} %copy.140, s32[1024]{0:T(1024)S(1)} %pad_clamp_fusion.3), kind=kCustom, calls=%fused_computation.clone | custom fusion | bytes 983808 | tf_op jit(solution)/shard_map/jit(_take)/gather | solution.py:55
  39.8 2.3 %select_bitcast_fusion.3 = f32[5,192,128]{2,0,1:T(8,128)} fusion(f32[192,5,128]{2,1,0:T(8,128)} %gather_fusion, pred[192]{0:T(512)(128)(4,1)S(1)} %compare_and_fusion.3), kind=kLoop, calls=%fused_computation.19 | loop fusion | flops 122880 | bytes 983232 | tf_op jit(solution)/shard_map/jit(_take)/select_n | solution.py:55
  42.1 9.3 %all-to-all-done.1 = f32[5,192,128]{2,0,1:T(8,128)S(1)} async-done(((f32[5,192,128]{2,0,1:T(8,128)}), f32[5,192,128]{2,0,1:T(8,128)S(1)}, u32[]{:S(2)}, u32[]{:S(2)}) %all-to-all-start.1) | async-done | bytes 491552 | tf_op jit(solution)/shard_map/all_to_all | solution.py:57
  51.4 4.3 %all-to-all-start = ((f32[5,192,128]{2,0,1:T(8,128)}), f32[5,192,128]{2,0,1:T(8,128)}, u32[]{:S(2)}, u32[]{:S(2)}) async-start(f32[5,192,128]{2,0,1:T(8,128)} %select_bitcast_fusion.3), calls=%async_computation | async-start | bytes 1572864 | tf_op jit(solution)/shard_map/all_to_all | solution.py:58
  56.9 5.6 %collective-permute-start.3 = (f32[5,192,3,1]{1,3,2,0:T(1,128)S(1)}, f32[5,192,3,1]{1,3,2,0:T(1,128)S(1)}, u32[]{:S(2)}, u32[]{:S(2)}) collective-permute-start(f32[5,192,3,1]{1,3,2,0:T(1,128)S(1)} %copy.151), channel_id=1, source_target_pairs={{1,0},{2,1},{3,2},{4,3},{5,4},{6,5},{7,6},{8,7},{9,8},{10,9},{11,1... | collective-permute-start | bytes 34568 | tf_op jit(solution)/shard_map/ppermute | solution.py:21
  63.1 1.9 %collective-permute-start.2 = (f32[5,192,3,1]{1,3,2,0:T(1,128)S(1)}, f32[5,192,3,1]{1,3,2,0:T(1,128)S(1)}, u32[]{:S(2)}, u32[]{:S(2)}) collective-permute-start(f32[5,192,3,1]{1,3,2,0:T(1,128)S(1)} %copy.149), channel_id=1, source_target_pairs={{0,1},{1,2},{2,3},{3,4},{4,5},{5,6},{6,7},{7,8},{8,9},{9,10},{10,1... | collective-permute-start | bytes 34568 | tf_op jit(solution)/shard_map/ppermute | solution.py:18
  66.5 3.8 %collective-permute-done.2 = f32[5,192,3,1]{1,3,2,0:T(1,128)S(1)} collective-permute-done((f32[5,192,3,1]{1,3,2,0:T(1,128)S(1)}, f32[5,192,3,1]{1,3,2,0:T(1,128)S(1)}, u32[]{:S(2)}, u32[]{:S(2)}) %collective-permute-start.2) | collective-permute-done | bytes 11552 | tf_op jit(solution)/shard_map/ppermute | solution.py:18
  70.8 2.7 %gather_fusion.3 = f32[192,5,128]{2,1,0:T(8,128)} fusion(f32[5,192,128]{2,0,1:T(8,128)} %copy-done.6, s32[1024]{0:T(1024)S(1)} %pad_clamp_fusion), kind=kCustom, calls=%fused_computation.3.clone | custom fusion | bytes 983808 | tf_op jit(solution)/shard_map/jit(_take)/gather | solution.py:60
  73.5 2.7 %gather_fusion.1 = f32[192,5,128]{2,1,0:T(8,128)} fusion(f32[5,192,128]{2,0,1:T(8,128)} %all-to-all-done, s32[1024]{0:T(1024)S(1)} %pad_clamp_fusion.2), kind=kCustom, calls=%fused_computation.1.clone | custom fusion | bytes 983808 | tf_op jit(solution)/shard_map/jit(_take)/gather | solution.py:66
  76.3 3.9 %fusion.7 = f32[5,192,1,128]{3,1,2,0:T(8,128)} fusion(f32[5,192,1,128]{3,1,2,0:T(8,128)} %bitcast.158, f32[5,192,1,128]{3,1,0,2:T(8,128)S(1)} %bitcast.152, f32[5,192,1,128]{3,1,0,2:T(8,128)} %copy-done.1, f32[5,192,3,1]{3,1,0,2:T(8,128)S(1)} %copy.152, f32[5,192,1,128]{3,1,0,2:T(8,128)} %bitcast.155, f32[5,192,1,128]{3,1,0,2:T(8,128)} %bitcast.157, ...), kind=kLoop, calls=%fused_computation.23 | loop fusion | flops 3317760 | bytes 3955668 | tf_op jit(solution)/shard_map/mul | solution.py:119
  80.2 3.2 %collective-permute-start.5 = (f32[5,192,1,128]{3,1,2,0:T(8,128)}, f32[5,192,1,128]{3,1,2,0:T(8,128)S(1)}, u32[]{:S(2)}, u32[]{:S(2)}) collective-permute-start(f32[5,192,1,128]{3,1,2,0:T(8,128)} %fusion.7), channel_id=1, source_target_pairs={{0,16},{16,32},{32,48},{48,64},{64,80},{80,96},{96,112},{112,128},... | collective-permute-start | bytes 1474568 | tf_op jit(solution)/shard_map/ppermute | solution.py:18
  83.4 8.1 %collective-permute-start.4 = (f32[5,192,1,128]{3,1,2,0:T(8,128)}, f32[5,192,1,128]{3,1,2,0:T(8,128)S(1)}, u32[]{:S(2)}, u32[]{:S(2)}) collective-permute-start(f32[5,192,1,128]{3,1,2,0:T(8,128)} %fusion.7), channel_id=1, source_target_pairs={{16,0},{32,16},{48,32},{64,48},{80,64},{96,80},{112,96},{128,112},... | collective-permute-start | bytes 1474568 | tf_op jit(solution)/shard_map/ppermute | solution.py:21
  91.5 17.4 %collective-permute-done.5 = f32[5,192,1,128]{3,1,2,0:T(8,128)S(1)} collective-permute-done((f32[5,192,1,128]{3,1,2,0:T(8,128)}, f32[5,192,1,128]{3,1,2,0:T(8,128)S(1)}, u32[]{:S(2)}, u32[]{:S(2)}) %collective-permute-start.5) | collective-permute-done | bytes 491552 | tf_op jit(solution)/shard_map/ppermute | solution.py:18
  111.3 5.0 %all-to-all-start.3 = ((f32[5,192,128]{2,0,1:T(8,128)}), f32[5,192,128]{2,0,1:T(8,128)S(1)}, u32[]{:S(2)}, u32[]{:S(2)}) async-start(f32[5,192,128]{2,0,1:T(8,128)} %select_bitcast_fusion), calls=%async_computation.3 | async-start | bytes 1572864 | tf_op jit(solution)/shard_map/all_to_all | solution.py:57
  117.6 1.8 %gather_fusion.4 = f32[192,5,128]{2,1,0:T(8,128)S(1)} fusion(f32[5,192,128]{2,0,1:T(8,128)} %copy.162, s32[1024]{0:T(1024)S(1)} %pad_clamp_fusion.3), kind=kCustom, calls=%fused_computation.4.clone | custom fusion | bytes 983808 | tf_op jit(solution)/shard_map/jit(_take)/gather | solution.py:55
  120.6 9.4 %all-to-all-done.3 = f32[5,192,128]{2,0,1:T(8,128)S(1)} async-done(((f32[5,192,128]{2,0,1:T(8,128)}), f32[5,192,128]{2,0,1:T(8,128)S(1)}, u32[]{:S(2)}, u32[]{:S(2)}) %all-to-all-start.3) | async-done | bytes 491552 | tf_op jit(solution)/shard_map/all_to_all | solution.py:57
  130.0 4.5 %all-to-all-start.2 = ((f32[5,192,128]{2,0,1:T(8,128)}), f32[5,192,128]{2,0,1:T(8,128)}, u32[]{:S(2)}, u32[]{:S(2)}) async-start(f32[5,192,128]{2,0,1:T(8,128)} %select_bitcast_fusion.1), calls=%async_computation.2 | async-start | bytes 1572864 | tf_op jit(solution)/shard_map/all_to_all | solution.py:58
  136.8 5.4 %collective-permute-start.7 = (f32[5,192,3,1]{1,3,2,0:T(1,128)S(1)}, f32[5,192,3,1]{1,3,2,0:T(1,128)S(1)}, u32[]{:S(2)}, u32[]{:S(2)}) collective-permute-start(f32[5,192,3,1]{1,3,2,0:T(1,128)S(1)} %copy.170), channel_id=1, source_target_pairs={{1,0},{2,1},{3,2},{4,3},{5,4},{6,5},{7,6},{8,7},{9,8},{10,9},{11,1... | collective-permute-start | bytes 34568 | tf_op jit(solution)/shard_map/ppermute | solution.py:21
  142.8 1.9 %collective-permute-start.6 = (f32[5,192,3,1]{1,3,2,0:T(1,128)S(1)}, f32[5,192,3,1]{1,3,2,0:T(1,128)S(1)}, u32[]{:S(2)}, u32[]{:S(2)}) collective-permute-start(f32[5,192,3,1]{1,3,2,0:T(1,128)S(1)} %copy.168), channel_id=1, source_target_pairs={{0,1},{1,2},{2,3},{3,4},{4,5},{5,6},{6,7},{7,8},{8,9},{9,10},{10,1... | collective-permute-start | bytes 34568 | tf_op jit(solution)/shard_map/ppermute | solution.py:18
  145.2 4.7 %collective-permute-done.6 = f32[5,192,3,1]{1,3,2,0:T(1,128)S(1)} collective-permute-done((f32[5,192,3,1]{1,3,2,0:T(1,128)S(1)}, f32[5,192,3,1]{1,3,2,0:T(1,128)S(1)}, u32[]{:S(2)}, u32[]{:S(2)}) %collective-permute-start.6) | collective-permute-done | bytes 11552 | tf_op jit(solution)/shard_map/ppermute | solution.py:18
  150.4 2.7 %gather_fusion.7 = f32[192,5,128]{2,1,0:T(8,128)} fusion(f32[5,192,128]{2,0,1:T(8,128)} %copy-done.7, s32[1024]{0:T(1024)S(1)} %pad_clamp_fusion), kind=kCustom, calls=%fused_computation.7.clone | custom fusion | bytes 983808 | tf_op jit(solution)/shard_map/jit(_take)/gather | solution.py:60
  153.2 2.7 %gather_fusion.5 = f32[192,5,128]{2,1,0:T(8,128)} fusion(f32[5,192,128]{2,0,1:T(8,128)} %all-to-all-done.2, s32[1024]{0:T(1024)S(1)} %pad_clamp_fusion.2), kind=kCustom, calls=%fused_computation.5.clone | custom fusion | bytes 983808 | tf_op jit(solution)/shard_map/jit(_take)/gather | solution.py:66
  155.9 3.7 %fusion.20 = f32[5,192,1,128]{3,1,2,0:T(8,128)} fusion(f32[5,192,1,128]{3,1,2,0:T(8,128)} %fusion.7, f32[5,192,3,1]{3,1,2,0:T(8,128)S(1)} %copy.171, f32[5,192,1,128]{3,1,2,0:T(8,128)} %copy-done.5, f32[5,192,1,128]{3,1,2,0:T(8,128)} %copy-done.4, f32[5,192,3,1]{3,1,2,0:T(8,128)S(1)} %copy.169, f32[192,5,128]{2,1,0:T(8,128)} %gather_fusion.7, ...), kind=kLoop, calls=%fused_computation.37 | loop fusion | flops 3317760 | bytes 3464148 | tf_op jit(solution)/shard_map/add | solution.py:122
  (97 shorter events, 17.8 us)
Async XLA Ops:
  0.0 11.6 %copy-start.9 = (s32[3072]{0:T(1024)S(1)}, s32[3072]{0:T(1024)}, u32[]{:S(2)}) copy-start(s32[3072]{0:T(1024)} %param.12) | copy-start | bytes 36868
  1.9 53.7 %copy-start.1 = (f32[5,192,1,128]{3,1,0,2:T(8,128)}, f32[5,192,1,128]{3,1,0,2:T(8,128)S(1)}, u32[]{:S(2)}) copy-start(f32[5,192,1,128]{3,1,0,2:T(8,128)S(1)} %get-tuple-element.13) | copy-start | bytes 1474564
  1.9 35.7 %collective-permute-start = (f32[5,192,1,128]{3,1,2,0:T(8,128)}, f32[5,192,1,128]{3,1,2,0:T(8,128)S(1)}, u32[]{:S(2)}, u32[]{:S(2)}) collective-permute-start(f32[5,192,1,128]{3,1,2,0:T(8,128)} %get-tuple-element.12), channel_id=1, source_target_pairs={{16,0},{32,16},{48,32},{64,48},{80,64},{96,80},{112,96},{128,112},... | collective-permute-start | bytes 1474568 | tf_op jit(solution)/shard_map/ppermute | solution.py:21
  9.7 21.7 %collective-permute-start.1 = (f32[5,192,1,128]{3,1,2,0:T(8,128)}, f32[5,192,1,128]{3,1,2,0:T(8,128)S(1)}, u32[]{:S(2)}, u32[]{:S(2)}) collective-permute-start(f32[5,192,1,128]{3,1,2,0:T(8,128)} %get-tuple-element.12), channel_id=1, source_target_pairs={{0,16},{16,32},{32,48},{48,64},{64,80},{80,96},{96,112},{112,128},... | collective-permute-start | bytes 1474568 | tf_op jit(solution)/shard_map/ppermute | solution.py:18
  31.4 24.2 %copy-start.3 = (f32[5,192,1,128]{3,1,2,0:T(8,128)}, f32[5,192,1,128]{3,1,2,0:T(8,128)S(1)}, u32[]{:S(2)}) copy-start(f32[5,192,1,128]{3,1,2,0:T(8,128)S(1)} %collective-permute-done.1) | copy-start | bytes 1474564
  33.9 17.5 %all-to-all-start.1 = ((f32[5,192,128]{2,0,1:T(8,128)}), f32[5,192,128]{2,0,1:T(8,128)S(1)}, u32[]{:S(2)}, u32[]{:S(2)}) async-start(f32[5,192,128]{2,0,1:T(8,128)} %select_bitcast_fusion.2), calls=%async_computation.1 | async-start | bytes 1572864 | tf_op jit(solution)/shard_map/all_to_all | solution.py:57
  37.6 18.1 %copy-start.2 = (f32[5,192,1,128]{3,1,2,0:T(8,128)}, f32[5,192,1,128]{3,1,2,0:T(8,128)S(1)}, u32[]{:S(2)}) copy-start(f32[5,192,1,128]{3,1,2,0:T(8,128)S(1)} %collective-permute-done) | copy-start | bytes 1474564
  51.4 4.3 %copy-start.6 = (f32[5,192,128]{2,0,1:T(8,128)}, f32[5,192,128]{2,0,1:T(8,128)S(1)}, u32[]{:S(2)}) copy-start(f32[5,192,128]{2,0,1:T(8,128)S(1)} %all-to-all-done.1) | copy-start | bytes 1474564
  51.4 22.1 %all-to-all-start = ((f32[5,192,128]{2,0,1:T(8,128)}), f32[5,192,128]{2,0,1:T(8,128)}, u32[]{:S(2)}, u32[]{:S(2)}) async-start(f32[5,192,128]{2,0,1:T(8,128)} %select_bitcast_fusion.3), calls=%async_computation | async-start | bytes 1572864 | tf_op jit(solution)/shard_map/all_to_all | solution.py:58
  56.3 8.7 %copy-start.8 = (f32[5,3,64,1,128]{4,2,0,1,3:T(8,128)S(1)}, f32[5,3,64,1,128]{4,2,0,1,3:T(8,128)}, u32[]{:S(2)}) copy-start(f32[5,3,64,1,128]{4,2,0,1,3:T(8,128)} %fusion.3) | copy-start | bytes 1474564
  56.9 9.0 %collective-permute-start.3 = (f32[5,192,3,1]{1,3,2,0:T(1,128)S(1)}, f32[5,192,3,1]{1,3,2,0:T(1,128)S(1)}, u32[]{:S(2)}, u32[]{:S(2)}) collective-permute-start(f32[5,192,3,1]{1,3,2,0:T(1,128)S(1)} %copy.151), channel_id=1, source_target_pairs={{1,0},{2,1},{3,2},{4,3},{5,4},{6,5},{7,6},{8,7},{9,8},{10,9},{11,1... | collective-permute-start | bytes 34568 | tf_op jit(solution)/shard_map/ppermute | solution.py:21
  63.1 7.2 %collective-permute-start.2 = (f32[5,192,3,1]{1,3,2,0:T(1,128)S(1)}, f32[5,192,3,1]{1,3,2,0:T(1,128)S(1)}, u32[]{:S(2)}, u32[]{:S(2)}) collective-permute-start(f32[5,192,3,1]{1,3,2,0:T(1,128)S(1)} %copy.149), channel_id=1, source_target_pairs={{0,1},{1,2},{2,3},{3,4},{4,5},{5,6},{6,7},{7,8},{8,9},{9,10},{10,1... | collective-permute-start | bytes 34568 | tf_op jit(solution)/shard_map/ppermute | solution.py:18
  66.4 9.9 %copy-start = (f32[5,192,1,128]{3,2,1,0:T(1,128)S(1)}, f32[5,192,1,128]{3,2,1,0:T(1,128)}, u32[]{:S(2)}) copy-start(f32[5,192,1,128]{3,2,1,0:T(1,128)} %param.9) | copy-start | bytes 1474564
  66.4 9.8 %copy-start.10 = (f32[5]{0:T(128)S(1)}, f32[5]{0:T(128)}, u32[]{:S(2)}) copy-start(f32[5]{0:T(128)} %constant.95.clone) | copy-start | bytes 64
  66.4 9.8 %copy-start.11 = (f32[5]{0:T(128)S(1)}, f32[5]{0:T(128)}, u32[]{:S(2)}) copy-start(f32[5]{0:T(128)} %constant.105) | copy-start | bytes 64
  66.5 9.8 %copy-start.12 = (f32[5]{0:T(128)S(1)}, f32[5]{0:T(128)}, u32[]{:S(2)}) copy-start(f32[5]{0:T(128)} %constant.104) | copy-start | bytes 64
  66.5 9.8 %copy-start.13 = (f32[5]{0:T(128)S(1)}, f32[5]{0:T(128)}, u32[]{:S(2)}) copy-start(f32[5]{0:T(128)} %constant.102) | copy-start | bytes 64
  80.2 28.6 %collective-permute-start.5 = (f32[5,192,1,128]{3,1,2,0:T(8,128)}, f32[5,192,1,128]{3,1,2,0:T(8,128)S(1)}, u32[]{:S(2)}, u32[]{:S(2)}) collective-permute-start(f32[5,192,1,128]{3,1,2,0:T(8,128)} %fusion.7), channel_id=1, source_target_pairs={{0,16},{16,32},{32,48},{48,64},{64,80},{80,96},{96,112},{112,128},... | collective-permute-start | bytes 1474568 | tf_op jit(solution)/shard_map/ppermute | solution.py:18
  83.4 32.9 %collective-permute-start.4 = (f32[5,192,1,128]{3,1,2,0:T(8,128)}, f32[5,192,1,128]{3,1,2,0:T(8,128)S(1)}, u32[]{:S(2)}, u32[]{:S(2)}) collective-permute-start(f32[5,192,1,128]{3,1,2,0:T(8,128)} %fusion.7), channel_id=1, source_target_pairs={{16,0},{32,16},{48,32},{64,48},{80,64},{96,80},{112,96},{128,112},... | collective-permute-start | bytes 1474568 | tf_op jit(solution)/shard_map/ppermute | solution.py:21
  108.9 25.6 %copy-start.4 = (f32[5,192,1,128]{3,1,2,0:T(8,128)}, f32[5,192,1,128]{3,1,2,0:T(8,128)S(1)}, u32[]{:S(2)}) copy-start(f32[5,192,1,128]{3,1,2,0:T(8,128)S(1)} %collective-permute-done.5) | copy-start | bytes 1474564
  111.3 18.7 %all-to-all-start.3 = ((f32[5,192,128]{2,0,1:T(8,128)}), f32[5,192,128]{2,0,1:T(8,128)S(1)}, u32[]{:S(2)}, u32[]{:S(2)}) async-start(f32[5,192,128]{2,0,1:T(8,128)} %select_bitcast_fusion), calls=%async_computation.3 | async-start | bytes 1572864 | tf_op jit(solution)/shard_map/all_to_all | solution.py:57
  116.3 18.2 %copy-start.5 = (f32[5,192,1,128]{3,1,2,0:T(8,128)}, f32[5,192,1,128]{3,1,2,0:T(8,128)S(1)}, u32[]{:S(2)}) copy-start(f32[5,192,1,128]{3,1,2,0:T(8,128)S(1)} %collective-permute-done.4) | copy-start | bytes 1474564
  130.0 4.5 %copy-start.7 = (f32[5,192,128]{2,0,1:T(8,128)}, f32[5,192,128]{2,0,1:T(8,128)S(1)}, u32[]{:S(2)}) copy-start(f32[5,192,128]{2,0,1:T(8,128)S(1)} %all-to-all-done.3) | copy-start | bytes 1474564
  130.0 23.1 %all-to-all-start.2 = ((f32[5,192,128]{2,0,1:T(8,128)}), f32[5,192,128]{2,0,1:T(8,128)}, u32[]{:S(2)}, u32[]{:S(2)}) async-start(f32[5,192,128]{2,0,1:T(8,128)} %select_bitcast_fusion.1), calls=%async_computation.2 | async-start | bytes 1572864 | tf_op jit(solution)/shard_map/all_to_all | solution.py:58
  136.8 8.0 %collective-permute-start.7 = (f32[5,192,3,1]{1,3,2,0:T(1,128)S(1)}, f32[5,192,3,1]{1,3,2,0:T(1,128)S(1)}, u32[]{:S(2)}, u32[]{:S(2)}) collective-permute-start(f32[5,192,3,1]{1,3,2,0:T(1,128)S(1)} %copy.170), channel_id=1, source_target_pairs={{1,0},{2,1},{3,2},{4,3},{5,4},{6,5},{7,6},{8,7},{9,8},{10,9},{11,1... | collective-permute-start | bytes 34568 | tf_op jit(solution)/shard_map/ppermute | solution.py:21
  142.8 7.2 %collective-permute-start.6 = (f32[5,192,3,1]{1,3,2,0:T(1,128)S(1)}, f32[5,192,3,1]{1,3,2,0:T(1,128)S(1)}, u32[]{:S(2)}, u32[]{:S(2)}) collective-permute-start(f32[5,192,3,1]{1,3,2,0:T(1,128)S(1)} %copy.168), channel_id=1, source_target_pairs={{0,1},{1,2},{2,3},{3,4},{4,5},{5,6},{6,7},{7,8},{8,9},{9,10},{10,1... | collective-permute-start | bytes 34568 | tf_op jit(solution)/shard_map/ppermute | solution.py:18
where the time goes:
time: 161 us; the launch traced here: 160 us
  starting transfers between devices  53.3 us (33%)
  waiting for transfers between devices  44.7 us (28%)
  local copies, waits for them, and re-layouts  30.7 us (19%)
  other arithmetic  28.1 us (17%)
  matrix products  2.23 us (1%)
    ppermute x4, starting transfers between devices, with_halo(): lax.ppermute(lax.slice_in_dim(block, 0, width, axis=dim), axis, backward)  26.9 us
    ppermute x4, waiting for transfers between devices, with_halo(): lax.ppermute(lax.slice_in_dim(block, block.shape[dim] - width, None, axis...  25.9 us
    all_to_all x2, waiting for transfers between devices, plane_remap(): lax.all_to_all(outgoing[0], 'span', split_axis=1, concat_axis=1, tiled=True)  18.8 us
    another operation x4, other arithmetic  9.3 us
    ppermute x4, starting transfers between devices, with_halo(): lax.ppermute(lax.slice_in_dim(block, block.shape[dim] - width, None, axis...  8.91 us
    all_to_all x2, starting transfers between devices, plane_remap(): lax.all_to_all(outgoing[1], 'span', split_axis=1, concat_axis=1, tiled=True)  8.73 us
    all_to_all x2, starting transfers between devices, plane_remap(): lax.all_to_all(outgoing[0], 'span', split_axis=1, concat_axis=1, tiled=True)  8.72 us
    gather x2, local copies, waits for them, and re-layouts, plane_remap(): upper_mapped = jnp.take(got_upper, upper_pos, axis=1)  5.49 us
  transfers between devices with their start and end apart: 12, of which 5 were waited for; matrix products, arithmetic and copies ran while one was open for 29% of the time, Pallas kernels for 0%

commit v1 on v0

--- a/solution.py
+++ b/solution.py
@@ -54,7 +54,12 @@
     )
     outgoing = (jnp.take(lower_rim, send_lower, axis=1), jnp.take(upper_rim, send_upper, axis=1))
     got_lower, got_upper = (
-        lax.all_to_all(outgoing[0], "span", split_axis=1, concat_axis=1, tiled=True),
+        jnp.concatenate(
+            lax.all_to_all(
+                jnp.stack(jnp.split(outgoing[0], lax.axis_size("span"), axis=1)), "span", 0, 0
+            ),
+            axis=1,
+        ),
         lax.all_to_all(outgoing[1], "span", split_axis=1, concat_axis=1, tiled=True),
     )
     lower_mapped = jnp.take(got_lower, own_dev * capacity + own_arrival, axis=1)

time: 161 us -> 163 us (1.012)
  local copies, waits for them, and re-layouts: 30.7 us -> 37.1 us
  waiting for transfers between devices: 44.7 us -> 41.8 us
  other arithmetic: 28.1 us -> 26.3 us
    reshape x0 -> x2, local copies, waits for them, and re-layouts: none -> 4.39 us  [plane_remap(): jnp.concatenate(lax.all_to_all(jnp.stack(jnp.split(outgoing[0], lax.axis_...]
    all_to_all x2, waiting for transfers between devices: 18.8 us -> 15.9 us  [plane_remap(): lax.all_to_all(jnp.stack(jnp.split(outgoing[0], lax.axis_size('span'), ax...]
    another operation x3 -> x7, local copies, waits for them, and re-layouts: 2.49 us -> 4.37 us
    select_n x3, other arithmetic: 2.33 us -> 0.54 us  [plane_remap(): jnp.take(lower_rim, send_lower, axis=1)]
  transfers between devices with their start and end apart: 12 -> 12, of which waited for: 5 -> 5; matrix products, arithmetic and copies ran while one was open for 29% -> 31% of each run, Pallas kernels for 0% -> 0%
where the time goes in v1:
time: 163 us; the launch traced here: 162 us
  starting transfers between devices  53.3 us (33%)
  waiting for transfers between devices  41.8 us (26%)
  local copies, waits for them, and re-layouts  37.1 us (23%)
  other arithmetic  26.3 us (16%)
  matrix products  2.23 us (1%)
    ppermute x4, starting transfers between devices, with_halo(): lax.ppermute(lax.slice_in_dim(block, 0, width, axis=dim), axis, backward)  27.1 us
    ppermute x4, waiting for transfers between devices, with_halo(): lax.ppermute(lax.slice_in_dim(block, block.shape[dim] - width, None, axis...  25.9 us
    all_to_all x2, waiting for transfers between devices, plane_remap(): lax.all_to_all(jnp.stack(jnp.split(outgoing[0], lax.axis_size('span'), ax...  15.9 us
    another operation x4, other arithmetic  9.3 us
    ppermute x4, starting transfers between devices, with_halo(): lax.ppermute(lax.slice_in_dim(block, block.shape[dim] - width, None, axis...  8.91 us
    all_to_all x2, starting transfers between devices, plane_remap(): lax.all_to_all(jnp.stack(jnp.split(outgoing[0], lax.axis_size('span'), ax...  8.76 us
    all_to_all x2, starting transfers between devices, plane_remap(): lax.all_to_all(outgoing[1], 'span', split_axis=1, concat_axis=1, tiled=True)  8.57 us
    gather x2, local copies, waits for them, and re-layouts, plane_remap(): upper_mapped = jnp.take(got_upper, upper_pos, axis=1)  5.47 us
  transfers between devices with their start and end apart: 12, of which 5 were waited for; matrix products, arithmetic and copies ran while one was open for 31% of the time, Pallas kernels for 0%

profile of v1, /device:TPU:4, one launch (start us, length us, event | category | flops | bytes accessed | tf_op | source)
XLA Modules:
  0.0 161.7 jit_solution(13198108812575378885)
XLA Ops:
  0.0 1.9 %tanh_bitcast_fusion = (f32[5,192,1,128]{3,1,2,0:T(8,128)}, f32[5,192,1,128]{3,1,0,2:T(8,128)S(1)}) fusion(f32[5,192,1,128]{3,1,0,2:T(8,128)} %bitcast.283), kind=kLoop, calls=%fused_computation.177 | loop fusion | bytes 1474560 | tf_op jit(solution)/shard_map/tanh | solution.py:107
  1.9 7.8 %collective-permute-start = (f32[5,192,1,128]{3,1,2,0:T(8,128)}, f32[5,192,1,128]{3,1,2,0:T(8,128)S(1)}, u32[]{:S(2)}, u32[]{:S(2)}) collective-permute-start(f32[5,192,1,128]{3,1,2,0:T(8,128)} %get-tuple-element.12), channel_id=1, source_target_pairs={{16,0},{32,16},{48,32},{64,48},{80,64},{96,80},{112,96},{128,112},... | collective-permute-start | bytes 1474568 | tf_op jit(solution)/shard_map/ppermute | solution.py:21
  9.7 1.9 %collective-permute-start.1 = (f32[5,192,1,128]{3,1,2,0:T(8,128)}, f32[5,192,1,128]{3,1,2,0:T(8,128)S(1)}, u32[]{:S(2)}, u32[]{:S(2)}) collective-permute-start(f32[5,192,1,128]{3,1,2,0:T(8,128)} %get-tuple-element.12), channel_id=1, source_target_pairs={{0,16},{16,32},{32,48},{48,64},{64,80},{80,96},{96,112},{112,128},... | collective-permute-start | bytes 1474568 | tf_op jit(solution)/shard_map/ppermute | solution.py:18
  11.9 9.1 %reduce-window.6 = s32[16,16,2,128]{3,1,2,0:T(8,128)S(1)} reduce-window(s32[16,16,2,128]{3,1,2,0:T(8,128)S(1)} %copy_bitcast_fusion, s32[]{:T(128)} %constant.84.clone.1), window={size=1x1x1x128 pad=0_0x0_0x0_0x127_0}, to_apply=%region_0.1 | reduce-window | flops 8323072 | bytes 524292 | tf_op jit(solution)/shard_map/reduce-window
  22.8 2.5 %reshape.175 = bf16[3,5,64,5,64]{4,3,2,1,0:T(8,128)(2,1)S(1)} reshape(bf16[1,3,320,320]{3,2,1,0:T(8,128)(2,1)} %param.11) | data formatting | bytes 1228800 | tf_op jit(solution)/shard_map/reshape.12
  29.2 2.2 %fusion.3 = f32[5,3,64,1,128]{4,2,0,1,3:T(8,128)} fusion(bf16[3,5,64,5,64]{4,3,2,1,0:T(8,128)(2,1)S(1)} %reshape.175, bf16[5,3,64,128,1]{3,2,1,0,4:T(8,128)(2,1)} %bitcast.295), kind=kOutput, calls=%fused_computation.15 | convolution fusion | flops 78643200 | bytes 1351680 | tf_op jit(solution)/shard_map/sbclem,cblsp->ebmsp/dot_general | solution.py:121
  34.2 3.7 %all-to-all-start.1 = ((f32[16,5,12,128]{3,2,1,0:T(8,128)}), f32[16,5,12,128]{3,2,1,0:T(8,128)S(1)}, u32[]{:S(2)}, u32[]{:S(2)}) async-start(f32[16,5,12,128]{3,2,1,0:T(8,128)} %copy.168), calls=%async_computation.1 | async-start | bytes 1310720 | tf_op jit(solution)/shard_map/all_to_all | solution.py:58
  38.3 1.8 %gather_fusion = f32[192,5,128]{2,1,0:T(8,128)} fusion(f32[5,192,128]{2,0,1:T(8,128)S(1)} %copy.162, s32[1024]{0:T(1024)S(1)} %pad_clamp_fusion.3), kind=kCustom, calls=%fused_computation.clone | custom fusion | bytes 983808 | tf_op jit(solution)/shard_map/jit(_take)/gather | solution.py:55
  40.1 2.3 %select_bitcast_fusion.3 = f32[5,192,128]{2,0,1:T(8,128)} fusion(f32[192,5,128]{2,1,0:T(8,128)} %gather_fusion, pred[192]{0:T(512)(128)(4,1)S(1)} %compare_and_fusion.3), kind=kLoop, calls=%fused_computation.19 | loop fusion | flops 122880 | bytes 983232 | tf_op jit(solution)/shard_map/jit(_take)/select_n | solution.py:55
  42.4 7.9 %all-to-all-done.1 = f32[16,5,12,128]{3,2,1,0:T(8,128)S(1)} async-done(((f32[16,5,12,128]{3,2,1,0:T(8,128)}), f32[16,5,12,128]{3,2,1,0:T(8,128)S(1)}, u32[]{:S(2)}, u32[]{:S(2)}) %all-to-all-start.1) | async-done | bytes 491552 | tf_op jit(solution)/shard_map/all_to_all | solution.py:58
  50.2 4.3 %all-to-all-start = ((f32[5,192,128]{2,0,1:T(8,128)}), f32[5,192,128]{2,0,1:T(8,128)}, u32[]{:S(2)}, u32[]{:S(2)}) async-start(f32[5,192,128]{2,0,1:T(8,128)} %select_bitcast_fusion.3), calls=%async_computation | async-start | bytes 1572864 | tf_op jit(solution)/shard_map/all_to_all | solution.py:63
  55.8 5.6 %collective-permute-start.3 = (f32[5,192,3,1]{1,3,2,0:T(1,128)S(1)}, f32[5,192,3,1]{1,3,2,0:T(1,128)S(1)}, u32[]{:S(2)}, u32[]{:S(2)}) collective-permute-start(f32[5,192,3,1]{1,3,2,0:T(1,128)S(1)} %copy.176), channel_id=1, source_target_pairs={{1,0},{2,1},{3,2},{4,3},{5,4},{6,5},{7,6},{8,7},{9,8},{10,9},{11,1... | collective-permute-start | bytes 34568 | tf_op jit(solution)/shard_map/ppermute | solution.py:21
  62.0 1.9 %collective-permute-start.2 = (f32[5,192,3,1]{1,3,2,0:T(1,128)S(1)}, f32[5,192,3,1]{1,3,2,0:T(1,128)S(1)}, u32[]{:S(2)}, u32[]{:S(2)}) collective-permute-start(f32[5,192,3,1]{1,3,2,0:T(1,128)S(1)} %copy.174), channel_id=1, source_target_pairs={{0,1},{1,2},{2,3},{3,4},{4,5},{5,6},{6,7},{7,8},{8,9},{9,10},{10,1... | collective-permute-start | bytes 34568 | tf_op jit(solution)/shard_map/ppermute | solution.py:18
  65.3 3.9 %collective-permute-done.2 = f32[5,192,3,1]{1,3,2,0:T(1,128)S(1)} collective-permute-done((f32[5,192,3,1]{1,3,2,0:T(1,128)S(1)}, f32[5,192,3,1]{1,3,2,0:T(1,128)S(1)}, u32[]{:S(2)}, u32[]{:S(2)}) %collective-permute-start.2) | collective-permute-done | bytes 11552 | tf_op jit(solution)/shard_map/ppermute | solution.py:18
  69.7 2.2 %copy.205 = f32[5,16,12,128]{3,0,2,1:T(8,128)} copy(f32[5,16,12,128]{3,2,0,1:T(8,128)} %bitcast.290) | data formatting | bytes 983040 | tf_op jit(solution)/shard_map/reshape | solution.py:57
  71.9 2.7 %gather_fusion.3 = f32[192,5,128]{2,1,0:T(8,128)} fusion(f32[5,192,128]{2,0,1:T(8,128)} %bitcast.293, s32[1024]{0:T(1024)S(1)} %get-tuple-element.16), kind=kCustom, calls=%fused_computation.3.clone | custom fusion | bytes 983808 | tf_op jit(solution)/shard_map/jit(_take)/gather | solution.py:65
  74.6 2.7 %gather_fusion.1 = f32[192,5,128]{2,1,0:T(8,128)} fusion(f32[5,192,128]{2,0,1:T(8,128)} %all-to-all-done, s32[1024]{0:T(1024)S(1)} %get-tuple-element.17), kind=kCustom, calls=%fused_computation.1.clone | custom fusion | bytes 983808 | tf_op jit(solution)/shard_map/jit(_take)/gather | solution.py:71
  77.4 3.9 %fusion.7 = f32[5,192,1,128]{3,1,2,0:T(8,128)} fusion(f32[5,192,1,128]{3,1,2,0:T(8,128)} %bitcast.294, f32[5,192,1,128]{3,1,0,2:T(8,128)S(1)} %bitcast.284, f32[5,192,1,128]{3,1,0,2:T(8,128)} %copy-done.1, f32[5,192,3,1]{3,1,0,2:T(8,128)S(1)} %copy.177, f32[5,192,1,128]{3,1,0,2:T(8,128)} %bitcast.287, f32[5,192,1,128]{3,1,0,2:T(8,128)} %bitcast.289, ...), kind=kLoop, calls=%fused_computation.23 | loop fusion | flops 3317760 | bytes 3955668 | tf_op jit(solution)/shard_map/mul | solution.py:124
  81.3 3.2 %collective-permute-start.5 = (f32[5,192,1,128]{3,1,2,0:T(8,128)}, f32[5,192,1,128]{3,1,2,0:T(8,128)S(1)}, u32[]{:S(2)}, u32[]{:S(2)}) collective-permute-start(f32[5,192,1,128]{3,1,2,0:T(8,128)} %fusion.7), channel_id=1, source_target_pairs={{0,16},{16,32},{32,48},{48,64},{64,80},{80,96},{96,112},{112,128},... | collective-permute-start | bytes 1474568 | tf_op jit(solution)/shard_map/ppermute | solution.py:18
  84.5 8.1 %collective-permute-start.4 = (f32[5,192,1,128]{3,1,2,0:T(8,128)}, f32[5,192,1,128]{3,1,2,0:T(8,128)S(1)}, u32[]{:S(2)}, u32[]{:S(2)}) collective-permute-start(f32[5,192,1,128]{3,1,2,0:T(8,128)} %fusion.7), channel_id=1, source_target_pairs={{16,0},{32,16},{48,32},{64,48},{80,64},{96,80},{112,96},{128,112},... | collective-permute-start | bytes 1474568 | tf_op jit(solution)/shard_map/ppermute | solution.py:21
  92.6 17.3 %collective-permute-done.5 = f32[5,192,1,128]{3,1,2,0:T(8,128)S(1)} collective-permute-done((f32[5,192,1,128]{3,1,2,0:T(8,128)}, f32[5,192,1,128]{3,1,2,0:T(8,128)S(1)}, u32[]{:S(2)}, u32[]{:S(2)}) %collective-permute-start.5) | collective-permute-done | bytes 491552 | tf_op jit(solution)/shard_map/ppermute | solution.py:18
  112.6 5.0 %all-to-all-start.3 = ((f32[16,5,12,128]{3,2,1,0:T(8,128)}), f32[16,5,12,128]{3,2,1,0:T(8,128)S(1)}, u32[]{:S(2)}, u32[]{:S(2)}) async-start(f32[16,5,12,128]{3,2,1,0:T(8,128)} %copy.191), calls=%async_computation.3 | async-start | bytes 1310720 | tf_op jit(solution)/shard_map/all_to_all | solution.py:58
  118.9 1.8 %gather_fusion.4 = f32[192,5,128]{2,1,0:T(8,128)S(1)} fusion(f32[5,192,128]{2,0,1:T(8,128)} %copy.187, s32[1024]{0:T(1024)S(1)} %pad_clamp_fusion.3), kind=kCustom, calls=%fused_computation.4.clone | custom fusion | bytes 983808 | tf_op jit(solution)/shard_map/jit(_take)/gather | solution.py:55
  121.9 8.0 %all-to-all-done.3 = f32[16,5,12,128]{3,2,1,0:T(8,128)S(1)} async-done(((f32[16,5,12,128]{3,2,1,0:T(8,128)}), f32[16,5,12,128]{3,2,1,0:T(8,128)S(1)}, u32[]{:S(2)}, u32[]{:S(2)}) %all-to-all-start.3) | async-done | bytes 491552 | tf_op jit(solution)/shard_map/all_to_all | solution.py:58
  129.9 4.3 %all-to-all-start.2 = ((f32[5,192,128]{2,0,1:T(8,128)}), f32[5,192,128]{2,0,1:T(8,128)}, u32[]{:S(2)}, u32[]{:S(2)}) async-start(f32[5,192,128]{2,0,1:T(8,128)} %select_bitcast_fusion.1), calls=%async_computation.2 | async-start | bytes 1572864 | tf_op jit(solution)/shard_map/all_to_all | solution.py:63
  136.5 5.6 %collective-permute-start.7 = (f32[5,192,3,1]{1,3,2,0:T(1,128)S(1)}, f32[5,192,3,1]{1,3,2,0:T(1,128)S(1)}, u32[]{:S(2)}, u32[]{:S(2)}) collective-permute-start(f32[5,192,3,1]{1,3,2,0:T(1,128)S(1)} %copy.198), channel_id=1, source_target_pairs={{1,0},{2,1},{3,2},{4,3},{5,4},{6,5},{7,6},{8,7},{9,8},{10,9},{11,1... | collective-permute-start | bytes 34568 | tf_op jit(solution)/shard_map/ppermute | solution.py:21
  142.7 1.9 %collective-permute-start.6 = (f32[5,192,3,1]{1,3,2,0:T(1,128)S(1)}, f32[5,192,3,1]{1,3,2,0:T(1,128)S(1)}, u32[]{:S(2)}, u32[]{:S(2)}) collective-permute-start(f32[5,192,3,1]{1,3,2,0:T(1,128)S(1)} %copy.196), channel_id=1, source_target_pairs={{0,1},{1,2},{2,3},{3,4},{4,5},{5,6},{6,7},{7,8},{8,9},{9,10},{10,1... | collective-permute-start | bytes 34568 | tf_op jit(solution)/shard_map/ppermute | solution.py:18
  145.1 4.7 %collective-permute-done.6 = f32[5,192,3,1]{1,3,2,0:T(1,128)S(1)} collective-permute-done((f32[5,192,3,1]{1,3,2,0:T(1,128)S(1)}, f32[5,192,3,1]{1,3,2,0:T(1,128)S(1)}, u32[]{:S(2)}, u32[]{:S(2)}) %collective-permute-start.6) | collective-permute-done | bytes 11552 | tf_op jit(solution)/shard_map/ppermute | solution.py:18
  150.3 2.2 %copy.208 = f32[5,16,12,128]{3,0,2,1:T(8,128)} copy(f32[5,16,12,128]{3,2,0,1:T(8,128)} %bitcast.291) | data formatting | bytes 983040 | tf_op jit(solution)/shard_map/reshape | solution.py:57
  152.5 2.7 %gather_fusion.7 = f32[192,5,128]{2,1,0:T(8,128)} fusion(f32[5,192,128]{2,0,1:T(8,128)} %bitcast.292, s32[1024]{0:T(1024)S(1)} %get-tuple-element.16), kind=kCustom, calls=%fused_computation.7.clone | custom fusion | bytes 983808 | tf_op jit(solution)/shard_map/jit(_take)/gather | solution.py:65
  155.2 2.7 %gather_fusion.5 = f32[192,5,128]{2,1,0:T(8,128)} fusion(f32[5,192,128]{2,0,1:T(8,128)} %all-to-all-done.2, s32[1024]{0:T(1024)S(1)} %get-tuple-element.17), kind=kCustom, calls=%fused_computation.5.clone | custom fusion | bytes 983808 | tf_op jit(solution)/shard_map/jit(_take)/gather | solution.py:71
  158.0 3.7 %fusion.20 = f32[5,192,1,128]{3,1,2,0:T(8,128)} fusion(f32[5,192,1,128]{3,1,2,0:T(8,128)} %fusion.7, f32[5,192,3,1]{3,1,2,0:T(8,128)S(1)} %copy.199, f32[5,192,1,128]{3,1,2,0:T(8,128)} %copy-done.5, f32[5,192,1,128]{3,1,2,0:T(8,128)} %copy-done.4, f32[5,192,3,1]{3,1,2,0:T(8,128)S(1)} %copy.197, f32[192,5,128]{2,1,0:T(8,128)} %gather_fusion.7, ...), kind=kLoop, calls=%fused_computation.37 | loop fusion | flops 3317760 | bytes 3464148 | tf_op jit(solution)/shard_map/add | solution.py:127
  (133 shorter events, 21.1 us)
Async XLA Ops:
  0.0 11.6 %copy-start.9 = (s32[3072]{0:T(1024)S(1)}, s32[3072]{0:T(1024)}, u32[]{:S(2)}) copy-start(s32[3072]{0:T(1024)} %param.12) | copy-start | bytes 36868
  1.9 52.6 %copy-start.1 = (f32[5,192,1,128]{3,1,0,2:T(8,128)}, f32[5,192,1,128]{3,1,0,2:T(8,128)S(1)}, u32[]{:S(2)}) copy-start(f32[5,192,1,128]{3,1,0,2:T(8,128)S(1)} %get-tuple-element.13) | copy-start | bytes 1474564
  1.9 36.0 %collective-permute-start = (f32[5,192,1,128]{3,1,2,0:T(8,128)}, f32[5,192,1,128]{3,1,2,0:T(8,128)S(1)}, u32[]{:S(2)}, u32[]{:S(2)}) collective-permute-start(f32[5,192,1,128]{3,1,2,0:T(8,128)} %get-tuple-element.12), channel_id=1, source_target_pairs={{16,0},{32,16},{48,32},{64,48},{80,64},{96,80},{112,96},{128,112},... | collective-permute-start | bytes 1474568 | tf_op jit(solution)/shard_map/ppermute | solution.py:21
  9.7 21.7 %collective-permute-start.1 = (f32[5,192,1,128]{3,1,2,0:T(8,128)}, f32[5,192,1,128]{3,1,2,0:T(8,128)S(1)}, u32[]{:S(2)}, u32[]{:S(2)}) collective-permute-start(f32[5,192,1,128]{3,1,2,0:T(8,128)} %get-tuple-element.12), channel_id=1, source_target_pairs={{0,16},{16,32},{32,48},{48,64},{64,80},{80,96},{96,112},{112,128},... | collective-permute-start | bytes 1474568 | tf_op jit(solution)/shard_map/ppermute | solution.py:18
  31.5 23.1 %copy-start.3 = (f32[5,192,1,128]{3,1,2,0:T(8,128)}, f32[5,192,1,128]{3,1,2,0:T(8,128)S(1)}, u32[]{:S(2)}) copy-start(f32[5,192,1,128]{3,1,2,0:T(8,128)S(1)} %collective-permute-done.1) | copy-start | bytes 1474564
  34.2 16.1 %all-to-all-start.1 = ((f32[16,5,12,128]{3,2,1,0:T(8,128)}), f32[16,5,12,128]{3,2,1,0:T(8,128)S(1)}, u32[]{:S(2)}, u32[]{:S(2)}) async-start(f32[16,5,12,128]{3,2,1,0:T(8,128)} %copy.168), calls=%async_computation.1 | async-start | bytes 1310720 | tf_op jit(solution)/shard_map/all_to_all | solution.py:58
  37.9 16.6 %copy-start.2 = (f32[5,192,1,128]{3,1,2,0:T(8,128)}, f32[5,192,1,128]{3,1,2,0:T(8,128)S(1)}, u32[]{:S(2)}) copy-start(f32[5,192,1,128]{3,1,2,0:T(8,128)S(1)} %collective-permute-done) | copy-start | bytes 1474564
  50.2 4.3 %copy-start.6 = (f32[16,5,12,128]{3,2,1,0:T(8,128)}, f32[16,5,12,128]{3,2,1,0:T(8,128)S(1)}, u32[]{:S(2)}) copy-start(f32[16,5,12,128]{3,2,1,0:T(8,128)S(1)} %all-to-all-done.1) | copy-start | bytes 1474564
  50.2 24.4 %all-to-all-start = ((f32[5,192,128]{2,0,1:T(8,128)}), f32[5,192,128]{2,0,1:T(8,128)}, u32[]{:S(2)}, u32[]{:S(2)}) async-start(f32[5,192,128]{2,0,1:T(8,128)} %select_bitcast_fusion.3), calls=%async_computation | async-start | bytes 1572864 | tf_op jit(solution)/shard_map/all_to_all | solution.py:63
  55.2 8.7 %copy-start.8 = (f32[5,3,64,1,128]{4,2,0,1,3:T(8,128)S(1)}, f32[5,3,64,1,128]{4,2,0,1,3:T(8,128)}, u32[]{:S(2)}) copy-start(f32[5,3,64,1,128]{4,2,0,1,3:T(8,128)} %fusion.3) | copy-start | bytes 1474564
  55.8 9.0 %collective-permute-start.3 = (f32[5,192,3,1]{1,3,2,0:T(1,128)S(1)}, f32[5,192,3,1]{1,3,2,0:T(1,128)S(1)}, u32[]{:S(2)}, u32[]{:S(2)}) collective-permute-start(f32[5,192,3,1]{1,3,2,0:T(1,128)S(1)} %copy.176), channel_id=1, source_target_pairs={{1,0},{2,1},{3,2},{4,3},{5,4},{6,5},{7,6},{8,7},{9,8},{10,9},{11,1... | collective-permute-start | bytes 34568 | tf_op jit(solution)/shard_map/ppermute | solution.py:21
  62.0 7.2 %collective-permute-start.2 = (f32[5,192,3,1]{1,3,2,0:T(1,128)S(1)}, f32[5,192,3,1]{1,3,2,0:T(1,128)S(1)}, u32[]{:S(2)}, u32[]{:S(2)}) collective-permute-start(f32[5,192,3,1]{1,3,2,0:T(1,128)S(1)} %copy.174), channel_id=1, source_target_pairs={{0,1},{1,2},{2,3},{3,4},{4,5},{5,6},{6,7},{7,8},{8,9},{9,10},{10,1... | collective-permute-start | bytes 34568 | tf_op jit(solution)/shard_map/ppermute | solution.py:18
  69.6 7.7 %copy-start = (f32[5,192,1,128]{3,2,1,0:T(1,128)S(1)}, f32[5,192,1,128]{3,2,1,0:T(1,128)}, u32[]{:S(2)}) copy-start(f32[5,192,1,128]{3,2,1,0:T(1,128)} %param.9) | copy-start | bytes 1474564
  69.6 7.7 %copy-start.10 = (f32[5]{0:T(128)S(1)}, f32[5]{0:T(128)}, u32[]{:S(2)}) copy-start(f32[5]{0:T(128)} %constant.95.clone) | copy-start | bytes 64
  69.7 7.7 %copy-start.11 = (f32[5]{0:T(128)S(1)}, f32[5]{0:T(128)}, u32[]{:S(2)}) copy-start(f32[5]{0:T(128)} %constant.105) | copy-start | bytes 64
  69.7 7.7 %copy-start.12 = (f32[5]{0:T(128)S(1)}, f32[5]{0:T(128)}, u32[]{:S(2)}) copy-start(f32[5]{0:T(128)} %constant.104) | copy-start | bytes 64
  69.7 7.7 %copy-start.13 = (f32[5]{0:T(128)S(1)}, f32[5]{0:T(128)}, u32[]{:S(2)}) copy-start(f32[5]{0:T(128)} %constant.102) | copy-start | bytes 64
  81.3 28.6 %collective-permute-start.5 = (f32[5,192,1,128]{3,1,2,0:T(8,128)}, f32[5,192,1,128]{3,1,2,0:T(8,128)S(1)}, u32[]{:S(2)}, u32[]{:S(2)}) collective-permute-start(f32[5,192,1,128]{3,1,2,0:T(8,128)} %fusion.7), channel_id=1, source_target_pairs={{0,16},{16,32},{32,48},{48,64},{64,80},{80,96},{96,112},{112,128},... | collective-permute-start | bytes 1474568 | tf_op jit(solution)/shard_map/ppermute | solution.py:18
  84.5 33.1 %collective-permute-start.4 = (f32[5,192,1,128]{3,1,2,0:T(8,128)}, f32[5,192,1,128]{3,1,2,0:T(8,128)S(1)}, u32[]{:S(2)}, u32[]{:S(2)}) collective-permute-start(f32[5,192,1,128]{3,1,2,0:T(8,128)} %fusion.7), channel_id=1, source_target_pairs={{16,0},{32,16},{48,32},{64,48},{80,64},{96,80},{112,96},{128,112},... | collective-permute-start | bytes 1474568 | tf_op jit(solution)/shard_map/ppermute | solution.py:21
  109.9 24.3 %copy-start.4 = (f32[5,192,1,128]{3,1,2,0:T(8,128)}, f32[5,192,1,128]{3,1,2,0:T(8,128)S(1)}, u32[]{:S(2)}) copy-start(f32[5,192,1,128]{3,1,2,0:T(8,128)S(1)} %collective-permute-done.5) | copy-start | bytes 1474564
  112.6 17.3 %all-to-all-start.3 = ((f32[16,5,12,128]{3,2,1,0:T(8,128)}), f32[16,5,12,128]{3,2,1,0:T(8,128)S(1)}, u32[]{:S(2)}, u32[]{:S(2)}) async-start(f32[16,5,12,128]{3,2,1,0:T(8,128)} %copy.191), calls=%async_computation.3 | async-start | bytes 1310720 | tf_op jit(solution)/shard_map/all_to_all | solution.py:58
  117.6 16.6 %copy-start.5 = (f32[5,192,1,128]{3,1,2,0:T(8,128)}, f32[5,192,1,128]{3,1,2,0:T(8,128)S(1)}, u32[]{:S(2)}) copy-start(f32[5,192,1,128]{3,1,2,0:T(8,128)S(1)} %collective-permute-done.4) | copy-start | bytes 1474564
  129.9 4.3 %copy-start.7 = (f32[16,5,12,128]{3,2,1,0:T(8,128)}, f32[16,5,12,128]{3,2,1,0:T(8,128)S(1)}, u32[]{:S(2)}) copy-start(f32[16,5,12,128]{3,2,1,0:T(8,128)S(1)} %all-to-all-done.3) | copy-start | bytes 1474564
  129.9 25.3 %all-to-all-start.2 = ((f32[5,192,128]{2,0,1:T(8,128)}), f32[5,192,128]{2,0,1:T(8,128)}, u32[]{:S(2)}, u32[]{:S(2)}) async-start(f32[5,192,128]{2,0,1:T(8,128)} %select_bitcast_fusion.1), calls=%async_computation.2 | async-start | bytes 1572864 | tf_op jit(solution)/shard_map/all_to_all | solution.py:63
  136.5 8.1 %collective-permute-start.7 = (f32[5,192,3,1]{1,3,2,0:T(1,128)S(1)}, f32[5,192,3,1]{1,3,2,0:T(1,128)S(1)}, u32[]{:S(2)}, u32[]{:S(2)}) collective-permute-start(f32[5,192,3,1]{1,3,2,0:T(1,128)S(1)} %copy.198), channel_id=1, source_target_pairs={{1,0},{2,1},{3,2},{4,3},{5,4},{6,5},{7,6},{8,7},{9,8},{10,9},{11,1... | collective-permute-start | bytes 34568 | tf_op jit(solution)/shard_map/ppermute | solution.py:21
  142.7 7.2 %collective-permute-start.6 = (f32[5,192,3,1]{1,3,2,0:T(1,128)S(1)}, f32[5,192,3,1]{1,3,2,0:T(1,128)S(1)}, u32[]{:S(2)}, u32[]{:S(2)}) collective-permute-start(f32[5,192,3,1]{1,3,2,0:T(1,128)S(1)} %copy.196), channel_id=1, source_target_pairs={{0,1},{1,2},{2,3},{3,4},{4,5},{5,6},{6,7},{7,8},{8,9},{9,10},{10,1... | collective-permute-start | bytes 34568 | tf_op jit(solution)/shard_map/ppermute | solution.py:18
